TPU v7x, 256 devices: a whole 4x4x8 slice. The times are simulated.
256 devices in a mesh: seq: 32 (over z, x_hi, core), tp: 8 (over x_lo, y).
Axes of the slice: x: 4 (x_hi: 2, x_lo: 2; x = x_hi * 2 + x_lo), y: 4, z: 8, core: 2. Of those that a mesh axis runs over, the one named last changes fastest.
Arguments:
- tokens: bfloat16 [8192, 2048], P('seq', 'tp'), may hold values from -6 to 6
- ctx_len: int32 [32], P('seq'), may hold values from 0 to 12288, as said below
- cache_kv: bfloat16 [32, 4096, 2, 2048], P('seq', None, None, 'tp'), may hold values from -80 to 80, as said below
- cache_pos: int32 [32, 4096], P('seq'), may hold values from -1 to 12287, as said below
- attn_gain: float32 [2048], replicated, may hold values from 0.5 to 1.5
- moe_gain: float32 [2048], replicated, may hold values from 0.5 to 1.5
- qkv_train: float32 [2048, 3, 2048], P('seq', None, 'tp'), may hold values from -0.125 to 0.125
- out_train: float32 [2048, 2048], P('seq', 'tp'), may hold values from -0.125 to 0.125
- router: bfloat16 [2048, 64], replicated, may hold values from -0.125 to 0.125
- routes: int32 [8192, 6], P('seq'), may hold values from 0 to 63, all different within a row; in each aligned block of 256 rows (0 to 255, 256 to 511, ...) at most 32 rows name the same one
- handed_half: int32 [32], replicated, may hold values from 0 to 1
- fresh_gu: float32 [32, 1408, 2, 2048], P('seq', 'tp'), may hold values from -0.125 to 0.125
- fresh_down: float32 [32, 1408, 2048], P('seq', 'tp'), may hold values from -0.15625 to 0.15625
- server_gu: bfloat16 [32, 2816, 2, 2048], P('seq', 'tp'), may hold values from -0.125 to 0.125
- server_down: bfloat16 [32, 2816, 2048], P('seq', 'tp'), may hold values from -0.15625 to 0.15625
Outputs:
- layer_out: bfloat16 [8192, 2048], P('seq', 'tp')
Inputs may be any that keep to these rules, and one draw needn't show every extreme that they name: `ctx_len`: some request has exactly 12288 cached positions and some has none. `cache_pos`: -1 marks an empty slot. With a context length L of at most 4096, slot s holds position s for s < L. With a longer context, slots below 4 hold positions 0 to 3 and the other slots hold positions L - 4092 to L - 1, each once. `routes`: each row names 6 different experts; in the rows of one request no expert is named by more than 32 rows, and in every draw some expert by exactly 32. `cache_kv`: keys already carry their position's rotation.
All inputs are finite; a program needn't handle non-finite values.
Results may differ from a plain program's by a relative error of at most 0.025.
Values may be sent and summed in bfloat16 or wider, within the bound.
A program may use at most 128 MiB of HBM per device.

v0:
```python
import jax
import jax.numpy as jnp
from jax import lax
from jax.sharding import PartitionSpec as P

HEAD_DIM = 128
SINK = 4
WIN = 4096


def swapped(array, axis, apart):
    return lax.ppermute(array, axis, [(i, i ^ 1 << apart) for i in range(lax.axis_size(axis))])


def normed(field, gain_vec):
    values_in = field.astype(jnp.float32)
    inv_rms = lax.rsqrt(jnp.mean(values_in * values_in, axis=-1, keepdims=True) + 1e-06)
    return (values_in * inv_rms * gain_vec).astype(jnp.bfloat16)


def rotate(field, positions):
    half_dim = field.shape[-1] // 2
    frequency = 10000.0 ** (-jnp.arange(half_dim, dtype=jnp.float32) / half_dim)
    angles = positions.astype(jnp.float32)[:, None] * frequency[None, :]
    cosine = jnp.cos(angles)[:, None, :]
    sine = jnp.sin(angles)[:, None, :]
    first_half = field[..., :half_dim]
    second_half = field[..., half_dim:]
    return jnp.concatenate(
        [first_half * cosine - second_half * sine, second_half * cosine + first_half * sine],
        axis=-1,
    )


def attend(queries, keys_new, values_new, cache_keys, cache_values, slot_pos, context):
    new_count = queries.shape[0]
    key_all = jnp.concatenate([cache_keys, keys_new], axis=0)
    value_all = jnp.concatenate([cache_values, values_new], axis=0)
    scores = jnp.einsum(
        "qhd,khd->hqk", queries, key_all, preferred_element_type=jnp.float32
    ) / jnp.sqrt(jnp.float32(HEAD_DIM))
    token_ids = jnp.arange(new_count, dtype=jnp.int32)
    positions = context + token_ids
    cache_ok = (slot_pos[None, :] >= 0) & (
        (slot_pos[None, :] < SINK) | (positions[:, None] - slot_pos[None, :] < WIN)
    )
    new_ok = token_ids[None, :] <= token_ids[:, None]
    allowed = jnp.concatenate([cache_ok, new_ok], axis=1)
    scores = jnp.where(allowed[None], scores, jnp.float32(-1e30))
    row_top = jnp.max(scores, axis=-1, keepdims=True)
    weights = jnp.exp(scores - row_top)
    row_total = jnp.sum(weights, axis=-1, keepdims=True)
    probability = (weights / row_total).astype(jnp.bfloat16)
    return jnp.einsum(
        "hqk,khd->qhd", probability, value_all, preferred_element_type=jnp.float32
    ).astype(jnp.bfloat16)


def body(
    tokens,
    ctx_len,
    cache_kv,
    cache_pos,
    attn_gain,
    moe_gain,
    qkv_train,
    out_train,
    router,
    routes,
    handed_half,
    fresh_gu,
    fresh_down,
    server_gu,
    server_down,
):
    seq_count = lax.axis_size("seq")
    tp_place = lax.axis_index("tp")
    seq_place = lax.axis_index("seq")
    full_tokens = lax.all_gather(tokens, "tp", axis=1, tiled=True)
    tok_rows = full_tokens.shape[0]
    model_width = full_tokens.shape[1]
    qkv_all, out_all = (
        lax.all_gather(qkv_train.astype(jnp.bfloat16), "seq", axis=0, tiled=True),
        lax.all_gather(out_train.astype(jnp.bfloat16), "seq", axis=0, tiled=True),
    )
    local_width = qkv_all.shape[2]
    heads_here = local_width // HEAD_DIM
    normed_x = normed(full_tokens, attn_gain)
    projected = jnp.dot(
        normed_x, qkv_all.reshape(model_width, 3 * local_width), preferred_element_type=jnp.float32
    )
    projected = projected.reshape(tok_rows, 3, heads_here, HEAD_DIM)
    context = ctx_len[0]
    positions = context + jnp.arange(tok_rows, dtype=jnp.int32)
    queries = rotate(projected[:, 0], positions).astype(jnp.bfloat16)
    keys_new = rotate(projected[:, 1], positions).astype(jnp.bfloat16)
    values_new = projected[:, 2].astype(jnp.bfloat16)
    slot_count = cache_kv.shape[1]
    cached = cache_kv[0].reshape(slot_count, 2, heads_here, HEAD_DIM)
    mixed_heads = attend(
        queries, keys_new, values_new, cached[:, 0], cached[:, 1], cache_pos[0], context
    )
    mixed_heads = mixed_heads.reshape(tok_rows, local_width)
    partial_out = lax.dot_general(
        mixed_heads, out_all, (((1,), (1,)), ((), ())), preferred_element_type=jnp.float32
    )
    attn_total = lax.psum(partial_out.astype(jnp.bfloat16), "tp").astype(jnp.float32)
    hidden_state = (full_tokens.astype(jnp.float32) + attn_total).astype(jnp.bfloat16)
    moe_in = normed(hidden_state, moe_gain)
    logits = jnp.dot(moe_in, router, preferred_element_type=jnp.float32)
    gate_values = jax.nn.sigmoid(jnp.take_along_axis(logits, routes, axis=1))
    expert_count = router.shape[1]
    top_count = routes.shape[1]
    capacity = tok_rows // 8
    flat_routes = routes.reshape(-1)
    onehot = (flat_routes[:, None] == jnp.arange(expert_count, dtype=jnp.int32)[None, :]).astype(
        jnp.int32
    )
    before = jnp.cumsum(onehot, axis=0) - onehot
    slot_rank = jnp.sum(before * onehot, axis=1)
    slot_index = flat_routes * capacity + slot_rank
    repeated = jnp.repeat(moe_in, top_count, axis=0)
    outgoing = (
        jnp.zeros((expert_count * capacity, model_width), jnp.bfloat16).at[slot_index].set(repeated)
    )
    per_device = expert_count // seq_count
    pair_count = per_device // 2
    outgoing = outgoing.reshape(seq_count, per_device, capacity, model_width)
    arrived = lax.all_to_all(outgoing, "seq", split_axis=0, concat_axis=0, tiled=True)
    parity = tp_place % 2
    own_gu = fresh_gu.astype(jnp.bfloat16)
    own_down = fresh_down.astype(jnp.bfloat16)
    other_gu, other_down = swapped((own_gu, own_down), "tp", 0)
    lower_first = parity == 0
    group_gu = jnp.where(
        lower_first,
        jnp.concatenate([own_gu, other_gu], axis=1),
        jnp.concatenate([other_gu, own_gu], axis=1),
    )
    group_down = jnp.where(
        lower_first,
        jnp.concatenate([own_down, other_down], axis=1),
        jnp.concatenate([other_down, own_down], axis=1),
    )
    local_half = lax.dynamic_slice_in_dim(handed_half, seq_place * pair_count, pair_count, 0)
    use_fresh = local_half == parity
    weights_gu = jnp.where(use_fresh[:, None, None, None], group_gu, server_gu)
    weights_down = jnp.where(use_fresh[:, None, None], group_down, server_down)
    arrived_pairs = arrived.reshape(seq_count, pair_count, 2, capacity, model_width)
    mine = lax.dynamic_index_in_dim(arrived_pairs, parity, 2, keepdims=False)
    pre_act = jnp.einsum("sqcd,qfgd->sqcgf", mine, weights_gu, preferred_element_type=jnp.float32)
    activated = (jax.nn.silu(pre_act[..., 0, :]) * pre_act[..., 1, :]).astype(jnp.bfloat16)
    partial_y = jnp.einsum(
        "sqcf,qfd->sqcd", activated, weights_down, preferred_element_type=jnp.float32
    )
    selector = (jnp.arange(2, dtype=jnp.int32) == parity).astype(jnp.float32)
    placed = partial_y[:, :, None] * selector[None, None, :, None, None]
    placed = placed.reshape(seq_count, per_device, capacity, model_width)
    summed = lax.psum_scatter(placed.astype(jnp.bfloat16), "tp", scatter_dimension=3, tiled=True)
    returned = lax.all_to_all(summed, "seq", split_axis=0, concat_axis=0, tiled=True)
    part_width = returned.shape[3]
    flat_back = returned.reshape(expert_count * capacity, part_width)
    picked = flat_back[slot_index].reshape(tok_rows, top_count, part_width)
    combined = jnp.sum(gate_values[:, :, None] * picked.astype(jnp.float32), axis=1)
    residual = lax.dynamic_slice_in_dim(hidden_state, tp_place * part_width, part_width, 1)
    return (residual.astype(jnp.float32) + combined).astype(jnp.bfloat16)


def solution(mesh):
    placed = (
        P("seq", "tp"),
        P("seq"),
        P("seq", None, None, "tp"),
        P("seq", None),
        P(),
        P(),
        P("seq", None, "tp"),
        P("seq", "tp"),
        P(),
        P("seq", None),
        P(),
        P("seq", "tp", None, None),
        P("seq", "tp", None),
        P("seq", "tp", None, None),
        P("seq", "tp", None),
    )
    return jax.shard_map(
        body, mesh=mesh, in_specs=placed, out_specs=P("seq", "tp"), check_vma=False
    )
```

profile of v0, /device:TPU:4, one launch (start us, length us, event | category | flops | bytes accessed | tf_op | source)
XLA Modules:
  0.0 695.0 jit_solution(49394141733792327)
XLA Ops:
  6.5 0.7 all-gather.4.cloned.1.call-update
  7.3 1.6 convert_element_type.97
  9.0 1.4 convert_element_type.103
  11.2 0.8 compare_reduce_fusion.1
  12.0 11.2 %copy.54 = bf16[1,4096,2,256]{1,3,2,0:T(8,128)(2,1)} copy(bf16[1,4096,2,256]{3,2,1,0:T(2,128)(2,1)} %param.17) | data formatting | bytes 8388608 | tf_op args[2]
  23.2 4.0 slice_bitcast_fusion
  27.2 2.4 copy.73
  29.6 0.3 multiply_cosine_fusion
  29.9 1.0 fusion.9
  31.1 20.9 %all-gather.4.cloned.1.call-done = bf16[256,2048]{1,0:T(8,128)(2,1)} async-done(((bf16[256,256]{1,0:T(8,128)(2,1)}), bf16[256,2048]{1,0:T(8,128)(2,1)}) %all-gather.4.cloned.1.call-update) | async-done | bytes 1048592 | tf_op jit(solution)/shard_map/all_gather | solution.py:79
  52.0 1.5 fusion.21
  53.6 83.9 %all-gather.6.cloned.1.call-done = bf16[2048,3,256]{2,0,1:T(8,128)(2,1)} async-done(((bf16[64,3,256]{2,0,1:T(8,128)(2,1)}), bf16[2048,3,256]{2,0,1:T(8,128)(2,1)}) %all-gather.6.cloned.1.call-update) | async-done | bytes 3145744 | tf_op jit(solution)/shard_map/all_gather | solution.py:83
  137.5 4.7 copy.55
  142.2 3.0 fusion.45
  145.3 0.7 copy-done.4
  146.1 0.1 copy.57
  146.2 5.3 multiply_select_fusion
  151.5 1.0 fusion.55
  152.5 2.3 exponential_reduce_fusion
  154.7 3.4 fusion.41
  158.2 56.9 %all-gather.8.cloned.1.call-done = bf16[2048,256]{1,0:T(8,128)(2,1)} async-done(((bf16[64,256]{1,0:T(8,128)(2,1)}), bf16[2048,256]{1,0:T(8,128)(2,1)}) %all-gather.8.cloned.1.call-update) | async-done | bytes 1048592 | tf_op jit(solution)/shard_map/all_gather | solution.py:84
  215.1 2.7 convolution_convert_fusion
  217.8 0.1 copy.63
  217.9 0.1 eq.53
  218.1 0.1 eq.49
  218.3 18.3 %reduce-window.6 = s32[64,12,128]{2,1,0:T(8,128)S(1)} reduce-window(s32[64,12,128]{2,1,0:T(8,128)S(1)} %fusion.51, s32[]{:T(128)} %constant.29.clone.1), window={size=1x1x128 pad=0_0x0_0x127_0}, to_apply=%region_5.6 | reduce-window | flops 12484608 | bytes 786436 | tf_op jit(solution)/shard_map/reduce-window
  236.6 0.2 slice.66
  236.8 0.3 copy.65
  237.1 0.1 copy.66
  237.2 0.1 copy.62
  237.3 0.1 mul.207
  237.5 0.2 broadcast_add_fusion
  237.7 0.2 fusion.54
  237.9 60.7 %all-reduce.2.cloned.1.call-done = bf16[256,2048]{1,0:T(8,128)(2,1)} async-done(((bf16[256,2048]{1,0:T(8,128)(2,1)}), bf16[256,2048]{1,0:T(8,128)(2,1)}) %all-reduce.2.cloned.1.call-update) | async-done | bytes 1048592 | tf_op jit(solution)/shard_map/psum | solution.py:107
  298.6 1.7 fusion.18
  300.4 1.0 copy-done.1
  301.3 0.3 fusion.20
  301.6 4.6 broadcast_in_dim.42
  306.3 11.1 %reshape.346 = bf16[1536,2048]{1,0:T(8,128)(2,1)} reshape(bf16[256,6,2048]{2,1,0:T(8,128)(2,1)} %broadcast_in_dim.42) | data formatting | bytes 12582912 | tf_op jit(solution)/shard_map/reshape | solution.py:122
  317.3 15.1 %scatter_custom_fusion = bf16[2048,2048]{1,0:T(8,128)(2,1)} fusion(s32[1536]{0:T(1024)S(1)} %fusion.59, bf16[1536,2048]{1,0:T(8,128)(2,1)} %reshape.346, bf16[]{:T(256)} %constant.85.clone.1), kind=kCustom, calls=%fused_computation.17 | custom fusion | bytes 8389120 | tf_op jit(solution)/shard_map/scatter | solution.py:124
  332.4 10.2 %all-to-all-start = ((bf16[32,2,32,2048]{3,2,1,0:T(8,128)(2,1)}), bf16[32,2,32,2048]{3,2,1,0:T(8,128)(2,1)}, u32[]{:S(2)}, u32[]{:S(2)}) async-start(bf16[32,2,32,2048]{3,2,1,0:T(8,128)(2,1)} %bitcast.87), calls=%async_computation | async-start | bytes 16777216 | tf_op jit(solution)/shard_map/all_to_all | solution.py:129
  342.6 0.3 reduce-scatter.2.cloned.1.call-start
  342.9 3.3 convert_element_type.111
  346.4 2.1 collective-permute-start
  348.5 0.6 dynamic_slice.9
  349.6 31.2 %collective-permute-done.1 = bf16[1,176,2,2048]{3,2,1,0:T(2,128)(2,1)} collective-permute-done((bf16[1,176,2,2048]{3,2,1,0:T(2,128)(2,1)S(1)}, bf16[1,176,2,2048]{3,2,1,0:T(2,128)(2,1)}, u32[]{:S(2)}, u32[]{:S(2)}) %collective-permute-start.1) | collective-permute-done | bytes 1441824 | tf_op jit(solution)/shard_map/ppermute | solution.py:12
  380.8 16.0 %fusion.10 = bf16[352,2,2048,1]{2,1,0,3:T(2,128)(2,1)} fusion(bf16[1,352,2,2048]{3,2,1,0:T(2,128)(2,1)} %param.28, pred[]{:T(512)} %bitcast.17, pred[]{:T(512)S(6)} %eq.48, bf16[1,176,2,2048]{3,2,1,0:T(2,128)(2,1)} %collective-permute-done.1, bf16[1,176,2,2048]{3,2,1,0:T(2,128)(2,1)S(1)} %convert_element_type.111), kind=kLoop, calls=%fused_computation.25 | loop fusion | flops 5767168 | bytes 8650754 | tf_op jit(solution)/shard_map/reshape.10
  396.8 128.1 %all-to-all-done = bf16[32,2,32,2048]{3,2,1,0:T(8,128)(2,1)} async-done(((bf16[32,2,32,2048]{3,2,1,0:T(8,128)(2,1)}), bf16[32,2,32,2048]{3,2,1,0:T(8,128)(2,1)}, u32[]{:S(2)}, u32[]{:S(2)}) %all-to-all-start) | async-done | bytes 8388640 | tf_op jit(solution)/shard_map/all_to_all | solution.py:129
  524.9 7.3 %fusion.25 = f32[32,1,32,2,352]{4,2,0,3,1:T(8,128)S(1)} fusion(bf16[32,2,32,2048]{3,2,1,0:T(8,128)(2,1)} %all-to-all-done, s32[]{:T(128)S(6)} %select_n.95, bf16[352,2,2048,1]{2,1,0,3:T(2,128)(2,1)} %fusion.10), kind=kOutput, calls=%fused_computation.45 | convolution fusion | flops 2952790016 | bytes 9961476 | tf_op jit(solution)/shard_map/sqcd,qfgd->sqcgf/dot_general | solution.py:151
  532.2 7.0 %convolution_bitcast_fusion = f32[32,32,2048]{2,1,0:T(8,128)} fusion(bf16[1,352,2048]{2,1,0:T(8,128)(2,1)S(1)} %copy-done.8, bf16[1,176,2048]{2,1,0:T(8,128)(2,1)} %collective-permute-done, bf16[1,176,2048]{2,1,0:T(8,128)(2,1)S(1)} %convert_element_type.110, pred[]{:T(512)S(6)} %eq.48, pred[]{:T(512)} %bitcast.17, f32[32,1,32,2,352]{4,2,0,3,1:T(8,128)S(1)} %fusion.25), kind=kOutput, calls=%fused_computation.13 | convolution fusion | flops 1485766656 | bytes 14155778 | tf_op jit(solution)/shard_map/sqcf,qfd->sqcd/dot_general | solution.py:153
  539.2 8.5 %multiply_convert_fusion = bf16[32,2,32,2048]{3,2,1,0:T(8,128)(2,1)} fusion(f32[2]{0:T(128)S(1)} %compare_convert_fusion, f32[32,32,2048]{2,1,0:T(8,128)} %convolution_bitcast_fusion), kind=kLoop, calls=%fused_computation.4 | loop fusion | flops 8388608 | bytes 16777224 | tf_op jit(solution)/shard_map/convert_element_type | solution.py:159
  547.8 94.4 %reduce-scatter.2.cloned.1.call-done = bf16[32,2,32,256]{3,2,1,0:T(8,128)(2,1)} async-done(((bf16[32,2,32,2048]{3,2,1,0:T(8,128)(2,1)}), bf16[32,2,32,256]{3,2,1,0:T(8,128)(2,1)}) %reduce-scatter.2.cloned.1.call-update) | async-done | bytes 1048592 | tf_op jit(solution)/shard_map/reduce_scatter | solution.py:159
  642.1 10.1 %all-to-all-start.1 = ((bf16[32,2,32,256]{3,2,1,0:T(8,128)(2,1)}), bf16[32,2,32,256]{3,2,1,0:T(8,128)(2,1)S(1)}, u32[]{:S(2)}, u32[]{:S(2)}) async-start(bf16[32,2,32,256]{3,2,1,0:T(8,128)(2,1)} %reduce-scatter.2.cloned.1.call-done), calls=%async_computation.2 | async-start | bytes 2097152 | tf_op jit(solution)/shard_map/all_to_all | solution.py:160
  652.3 0.1 copy.59
  652.5 0.1 reshape.336
  652.6 0.4 fusion.67
  653.1 12.7 %gather_fusion.1 = f32[1536]{0:T(1024)S(1)} fusion(f32[256,64]{0,1:T(8,128)S(1)} %fusion.67, s32[1536]{0:T(1024)S(1)} %reshape.336), kind=kCustom, calls=%fused_computation.1 | custom fusion | bytes 24576 | tf_op jit(solution)/shard_map/jit(take_along_axis)/gather | solution.py:111
  665.8 0.1 reshape.339
  666.0 0.1 copy.61
  666.2 15.0 %all-to-all-done.1 = bf16[32,2,32,256]{3,2,1,0:T(8,128)(2,1)S(1)} async-done(((bf16[32,2,32,256]{3,2,1,0:T(8,128)(2,1)}), bf16[32,2,32,256]{3,2,1,0:T(8,128)(2,1)S(1)}, u32[]{:S(2)}, u32[]{:S(2)}) %all-to-all-start.1) | async-done | bytes 1048608 | tf_op jit(solution)/shard_map/all_to_all | solution.py:160
  681.2 4.8 gather_fusion
  686.0 0.2 reshape.327
  686.2 0.7 multiply_reduce_fusion
  686.9 1.6 add_convert_fusion
  (49 shorter events, 0.9 us)
Async XLA Ops:
  6.5 646.1 %copy-start = (bf16[2048,64]{0,1:T(8,128)(2,1)S(1)}, bf16[2048,64]{0,1:T(8,128)(2,1)}, u32[]{:S(2)}) copy-start(bf16[2048,64]{0,1:T(8,128)(2,1)} %param.23) | copy-start | bytes 786436
  6.5 45.5 %all-gather.4.cloned.1.call-start = ((), (), s32[]{:S(2)}) async-start(), calls=%async_computation.3 | async-start | bytes 1179648 | tf_op jit(solution)/shard_map/all_gather | solution.py:79
  7.3 130.2 %all-gather.6.cloned.1.call-start = ((), (), s32[]{:S(2)}) async-start(), calls=%async_computation.4 | async-start | bytes 3244032 | tf_op jit(solution)/shard_map/all_gather | solution.py:83
  8.9 206.1 %all-gather.8.cloned.1.call-start = ((), (), s32[]{:S(2)}) async-start(), calls=%async_computation.5 | async-start | bytes 1081344 | tf_op jit(solution)/shard_map/all_gather | solution.py:84
  10.4 288.2 %all-reduce.2.cloned.1.call-start = ((), (), s32[]{:S(2)}) async-start(), calls=%async_computation.6 | async-start | bytes 2097152 | tf_op jit(solution)/shard_map/psum | solution.py:107
  27.2 2.8 copy-start.6
  53.5 88.7 %copy-start.2 = (bf16[256,2048]{1,0:T(8,128)(2,1)S(1)}, bf16[256,2048]{1,0:T(8,128)(2,1)}, u32[]{:S(2)}) copy-start(bf16[256,2048]{1,0:T(8,128)(2,1)} %all-gather.4.cloned.1.call-done) | copy-start | bytes 3145732
  53.5 88.6 %copy-start.9 = (f32[2048]{0:T(1024)S(1)}, f32[2048]{0:T(1024)}, u32[]{:S(2)}) copy-start(f32[2048]{0:T(1024)} %param.19) | copy-start | bytes 24580
  145.2 0.9 copy-start.4
  158.2 59.6 %copy-start.5 = (s32[256,6]{0,1:T(8,128)S(1)}, s32[256,6]{0,1:T(8,128)}, u32[]{:S(2)}) copy-start(s32[256,6]{0,1:T(8,128)} %param.24) | copy-start | bytes 18436
  236.8 64.6 %copy-start.7 = (f32[2048]{0:T(1024)S(1)}, f32[2048]{0:T(1024)}, u32[]{:S(2)}) copy-start(f32[2048]{0:T(1024)} %param.20) | copy-start | bytes 24580
  300.3 1.0 copy-start.1
  332.4 192.5 %all-to-all-start = ((bf16[32,2,32,2048]{3,2,1,0:T(8,128)(2,1)}), bf16[32,2,32,2048]{3,2,1,0:T(8,128)(2,1)}, u32[]{:S(2)}, u32[]{:S(2)}) async-start(bf16[32,2,32,2048]{3,2,1,0:T(8,128)(2,1)} %bitcast.87), calls=%async_computation | async-start | bytes 16777216 | tf_op jit(solution)/shard_map/all_to_all | solution.py:129
  342.6 5.9 copy-start.10
  342.6 299.6 %reduce-scatter.2.cloned.1.call-start = ((), (), s32[]{:S(2)}) async-start(), calls=%async_computation.7 | async-start | bytes 9437184 | tf_op jit(solution)/shard_map/reduce_scatter | solution.py:159
  342.9 3.4 copy-start.3
  346.1 34.6 %collective-permute-start.1 = (bf16[1,176,2,2048]{3,2,1,0:T(2,128)(2,1)S(1)}, bf16[1,176,2,2048]{3,2,1,0:T(2,128)(2,1)}, u32[]{:S(2)}, u32[]{:S(2)}) collective-permute-start(bf16[1,176,2,2048]{3,2,1,0:T(2,128)(2,1)S(1)} %convert_element_type.111), channel_id=1, source_target_pairs={{0,1},{1,0},{2,3},{3,2},{4,5},{5,4},{6,7},{7,6},{8,9},{9,8},{10,11... | collective-permute-start | bytes 4325384 | tf_op jit(solution)/shard_map/ppermute | solution.py:12
  346.4 185.8 %collective-permute-start = (bf16[1,176,2048]{2,1,0:T(8,128)(2,1)S(1)}, bf16[1,176,2048]{2,1,0:T(8,128)(2,1)}, u32[]{:S(2)}, u32[]{:S(2)}) collective-permute-start(bf16[1,176,2048]{2,1,0:T(8,128)(2,1)S(1)} %convert_element_type.110), channel_id=1, source_target_pairs={{0,1},{1,0},{2,3},{3,2},{4,5},{5,4},{6,7},{7,6},{8,9},{9,8},{10,11... | collective-permute-start | bytes 2162696 | tf_op jit(solution)/shard_map/ppermute | solution.py:12
  396.8 135.4 %copy-start.8 = (bf16[1,352,2048]{2,1,0:T(8,128)(2,1)S(1)}, bf16[1,352,2048]{2,1,0:T(8,128)(2,1)}, u32[]{:S(2)}) copy-start(bf16[1,352,2048]{2,1,0:T(8,128)(2,1)} %param.29) | copy-start | bytes 4325380
  642.1 39.1 %all-to-all-start.1 = ((bf16[32,2,32,256]{3,2,1,0:T(8,128)(2,1)}), bf16[32,2,32,256]{3,2,1,0:T(8,128)(2,1)S(1)}, u32[]{:S(2)}, u32[]{:S(2)}) async-start(bf16[32,2,32,256]{3,2,1,0:T(8,128)(2,1)} %reduce-scatter.2.cloned.1.call-done), calls=%async_computation.2 | async-start | bytes 2097152 | tf_op jit(solution)/shard_map/all_to_all | solution.py:160
Sparse Core Ops, SparseCore 0:
  9.1 42.8 all-gather.3
  54.8 82.6 all-gather.5
  140.3 74.7 all-gather.7
  217.9 80.6 all-reduce.1
  547.9 94.2 reduce-scatter.1
where the time goes:
time: 696 us; the launch traced here: 695 us
  waiting for transfers between devices  492 us (71%)
  local copies, waits for them, and re-layouts  76.1 us (11%)
  other arithmetic  60.2 us (9%)
  matrix products  29.2 us (4%)
  starting transfers between devices  22.9 us (3%)
  between operations  14.8 us (2%)
    all_to_all x1, waiting for transfers between devices, body(): lax.all_to_all(outgoing, 'seq', split_axis=0, concat_axis=0, tiled=True)  128 us
    reduce_scatter x1, waiting for transfers between devices, body(): lax.psum_scatter(placed.astype(jnp.bfloat16), 'tp', scatter_dimension=3,...  94.4 us
    all_gather x1, waiting for transfers between devices, body(): lax.all_gather(qkv_train.astype(jnp.bfloat16), 'seq', axis=0, tiled=True)  83.9 us
    psum x1, waiting for transfers between devices, body(): lax.psum(partial_out.astype(jnp.bfloat16), 'tp').astype(jnp.float32)  60.7 us
    all_gather x1, waiting for transfers between devices, body(): lax.all_gather(out_train.astype(jnp.bfloat16), 'seq', axis=0, tiled=True)  56.9 us
    another operation x5, other arithmetic  34.6 us
    ppermute x2, waiting for transfers between devices, swapped(): lax.ppermute(array, axis, [(i, i ^ 1 << apart) for i in range(lax.axis_si...  31.2 us
    all_gather x1, waiting for transfers between devices, body(): full_tokens = lax.all_gather(tokens, 'tp', axis=1, tiled=True)  20.9 us
  transfers between devices with their start and end apart: 9, of which 8 were waited for; matrix products, arithmetic and copies ran while one was open for 15% of the time, Pallas kernels for 0%

commit v1 on v0

--- a/solution.py
+++ b/solution.py
@@ -104,7 +104,11 @@
     partial_out = lax.dot_general(
         mixed_heads, out_all, (((1,), (1,)), ((), ())), preferred_element_type=jnp.float32
     )
-    attn_total = lax.psum(partial_out.astype(jnp.bfloat16), "tp").astype(jnp.float32)
+
+    def guide_stocks_now(mine_x, mesh_dim):
+        return lax.all_gather(mine_x, mesh_dim).sum(axis=0)
+
+    attn_total = guide_stocks_now(partial_out.astype(jnp.bfloat16), "tp").astype(jnp.float32)
     hidden_state = (full_tokens.astype(jnp.float32) + attn_total).astype(jnp.bfloat16)
     moe_in = normed(hidden_state, moe_gain)
     logits = jnp.dot(moe_in, router, preferred_element_type=jnp.float32)

time: 696 us -> 720 us (1.034); the launches traced: 695 us -> 711 us
  waiting for transfers between devices: 492 us -> 503 us
    all_gather x0 -> x1, waiting for transfers between devices: none -> 72.7 us  [guide_stocks_now(): return lax.all_gather(mine_x, mesh_dim).sum(axis=0)]
    psum x1 -> x0, waiting for transfers between devices: 60.7 us -> none  [body(): lax.psum(partial_out.astype(jnp.bfloat16), 'tp').astype(jnp.float32)]
where the time goes in v1:
time: 720 us; the launch traced here: 711 us
  waiting for transfers between devices  503 us (70%)
  local copies, waits for them, and re-layouts  76.2 us (11%)
  other arithmetic  64.5 us (9%)
  matrix products  29.2 us (4%)
  starting transfers between devices  22.9 us (3%)
  between operations  15 us (2%)
    all_to_all x1, waiting for transfers between devices, body(): lax.all_to_all(outgoing, 'seq', split_axis=0, concat_axis=0, tiled=True)  128 us
    reduce_scatter x1, waiting for transfers between devices, body(): lax.psum_scatter(placed.astype(jnp.bfloat16), 'tp', scatter_dimension=3,...  93.5 us
    all_gather x1, waiting for transfers between devices, body(): lax.all_gather(qkv_train.astype(jnp.bfloat16), 'seq', axis=0, tiled=True)  83.9 us
    all_gather x1, waiting for transfers between devices, guide_stocks_now(): return lax.all_gather(mine_x, mesh_dim).sum(axis=0)  72.7 us
    all_gather x1, waiting for transfers between devices, body(): lax.all_gather(out_train.astype(jnp.bfloat16), 'seq', axis=0, tiled=True)  56.9 us
    another operation x5, other arithmetic  34.9 us
    ppermute x2, waiting for transfers between devices, swapped(): lax.ppermute(array, axis, [(i, i ^ 1 << apart) for i in range(lax.axis_si...  31.2 us
    all_gather x1, waiting for transfers between devices, body(): full_tokens = lax.all_gather(tokens, 'tp', axis=1, tiled=True)  20.9 us
  transfers between devices with their start and end apart: 9, of which 8 were waited for; matrix products, arithmetic and copies ran while one was open for 15% of the time, Pallas kernels for 0%

profile of v1, /device:TPU:4, one launch (start us, length us, event | category | flops | bytes accessed | tf_op | source)
XLA Modules:
  0.0 711.1 jit_solution(16326851387398706127)
XLA Ops:
  6.5 0.7 all-gather.6.cloned.1.call-update
  7.3 1.6 convert_element_type.99
  9.0 1.4 convert_element_type.105
  11.2 0.8 compare_reduce_fusion.1
  12.0 11.2 %copy.54 = bf16[1,4096,2,256]{1,3,2,0:T(8,128)(2,1)} copy(bf16[1,4096,2,256]{3,2,1,0:T(2,128)(2,1)} %param.17) | data formatting | bytes 8388608 | tf_op args[2]
  23.2 4.0 slice_bitcast_fusion
  27.2 2.4 copy.73
  29.6 0.3 multiply_cosine_fusion
  29.9 1.0 fusion.9
  31.1 20.9 %all-gather.6.cloned.1.call-done = bf16[256,2048]{1,0:T(8,128)(2,1)} async-done(((bf16[256,256]{1,0:T(8,128)(2,1)}), bf16[256,2048]{1,0:T(8,128)(2,1)}) %all-gather.6.cloned.1.call-update) | async-done | bytes 1048592 | tf_op jit(solution)/shard_map/all_gather | solution.py:79
  52.0 1.5 fusion.21
  53.6 83.9 %all-gather.8.cloned.1.call-done = bf16[2048,3,256]{2,0,1:T(8,128)(2,1)} async-done(((bf16[64,3,256]{2,0,1:T(8,128)(2,1)}), bf16[2048,3,256]{2,0,1:T(8,128)(2,1)}) %all-gather.8.cloned.1.call-update) | async-done | bytes 3145744 | tf_op jit(solution)/shard_map/all_gather | solution.py:83
  137.5 4.7 copy.55
  142.2 3.0 fusion.45
  145.3 0.7 copy-done.4
  146.1 0.1 copy.57
  146.2 5.3 multiply_select_fusion
  151.5 1.0 fusion.55
  152.5 2.3 exponential_reduce_fusion
  154.7 3.4 fusion.41
  158.2 56.9 %all-gather.10.cloned.1.call-done = bf16[2048,256]{1,0:T(8,128)(2,1)} async-done(((bf16[64,256]{1,0:T(8,128)(2,1)}), bf16[2048,256]{1,0:T(8,128)(2,1)}) %all-gather.10.cloned.1.call-update) | async-done | bytes 1048592 | tf_op jit(solution)/shard_map/all_gather | solution.py:84
  215.1 2.8 convolution_convert_fusion
  217.9 0.1 copy.63
  218.0 0.1 eq.53
  218.2 0.1 eq.49
  218.3 18.6 %reduce-window.6 = s32[64,12,128]{2,1,0:T(8,128)S(1)} reduce-window(s32[64,12,128]{2,1,0:T(8,128)S(1)} %fusion.51, s32[]{:T(128)} %constant.36.clone.1), window={size=1x1x128 pad=0_0x0_0x127_0}, to_apply=%region_5.6 | reduce-window | flops 12484608 | bytes 786436 | tf_op jit(solution)/shard_map/reduce-window
  236.9 0.2 slice.66
  237.1 0.3 copy.65
  237.4 0.1 copy.66
  237.5 0.1 copy.62
  237.7 0.1 mul.207
  237.8 0.2 broadcast_add_fusion
  238.0 0.2 fusion.54
  238.3 72.7 %all-gather.12.cloned.1.call-done = bf16[2048,2048]{1,0:T(8,128)(2,1)} async-done(((bf16[256,2048]{1,0:T(8,128)(2,1)}), bf16[2048,2048]{1,0:T(8,128)(2,1)}) %all-gather.12.cloned.1.call-update) | async-done | bytes 8388624 | tf_op jit(solution)/shard_map/all_gather | solution.py:109
  310.9 5.2 reduce_sum.61
  316.2 0.5 fusion.18
  316.7 1.0 copy-done.1
  317.6 0.3 fusion.20
  318.0 4.6 broadcast_in_dim.42
  322.6 11.1 %reshape.346 = bf16[1536,2048]{1,0:T(8,128)(2,1)} reshape(bf16[256,6,2048]{2,1,0:T(8,128)(2,1)} %broadcast_in_dim.42) | data formatting | bytes 12582912 | tf_op jit(solution)/shard_map/reshape | solution.py:126
  333.6 15.2 %scatter_custom_fusion = bf16[2048,2048]{1,0:T(8,128)(2,1)} fusion(s32[1536]{0:T(1024)S(1)} %fusion.59, bf16[1536,2048]{1,0:T(8,128)(2,1)} %reshape.346, bf16[]{:T(256)} %constant.74.clone.1), kind=kCustom, calls=%fused_computation.17 | custom fusion | bytes 8389120 | tf_op jit(solution)/shard_map/scatter | solution.py:128
  348.9 10.2 %all-to-all-start = ((bf16[32,2,32,2048]{3,2,1,0:T(8,128)(2,1)}), bf16[32,2,32,2048]{3,2,1,0:T(8,128)(2,1)}, u32[]{:S(2)}, u32[]{:S(2)}) async-start(bf16[32,2,32,2048]{3,2,1,0:T(8,128)(2,1)} %bitcast.88), calls=%async_computation | async-start | bytes 16777216 | tf_op jit(solution)/shard_map/all_to_all | solution.py:133
  359.2 3.3 convert_element_type.113
  362.6 2.1 collective-permute-start
  364.7 0.6 dynamic_slice.9
  365.9 31.2 %collective-permute-done.1 = bf16[1,176,2,2048]{3,2,1,0:T(2,128)(2,1)} collective-permute-done((bf16[1,176,2,2048]{3,2,1,0:T(2,128)(2,1)S(1)}, bf16[1,176,2,2048]{3,2,1,0:T(2,128)(2,1)}, u32[]{:S(2)}, u32[]{:S(2)}) %collective-permute-start.1) | collective-permute-done | bytes 1441824 | tf_op jit(solution)/shard_map/ppermute | solution.py:12
  397.1 16.0 %fusion.10 = bf16[352,2,2048,1]{2,1,0,3:T(2,128)(2,1)} fusion(bf16[1,352,2,2048]{3,2,1,0:T(2,128)(2,1)} %param.28, pred[]{:T(512)} %bitcast.18, pred[]{:T(512)S(6)} %eq.48, bf16[1,176,2,2048]{3,2,1,0:T(2,128)(2,1)} %collective-permute-done.1, bf16[1,176,2,2048]{3,2,1,0:T(2,128)(2,1)S(1)} %convert_element_type.113), kind=kLoop, calls=%fused_computation.25 | loop fusion | flops 5767168 | bytes 8650754 | tf_op jit(solution)/shard_map/reshape.10
  413.1 128.3 %all-to-all-done = bf16[32,2,32,2048]{3,2,1,0:T(8,128)(2,1)} async-done(((bf16[32,2,32,2048]{3,2,1,0:T(8,128)(2,1)}), bf16[32,2,32,2048]{3,2,1,0:T(8,128)(2,1)}, u32[]{:S(2)}, u32[]{:S(2)}) %all-to-all-start) | async-done | bytes 8388640 | tf_op jit(solution)/shard_map/all_to_all | solution.py:133
  541.4 7.3 %fusion.25 = f32[32,1,32,2,352]{4,2,0,3,1:T(8,128)S(1)} fusion(bf16[32,2,32,2048]{3,2,1,0:T(8,128)(2,1)} %all-to-all-done, s32[]{:T(128)S(6)} %select_n.95, bf16[352,2,2048,1]{2,1,0,3:T(2,128)(2,1)} %fusion.10), kind=kOutput, calls=%fused_computation.45 | convolution fusion | flops 2952790016 | bytes 9961476 | tf_op jit(solution)/shard_map/sqcd,qfgd->sqcgf/dot_general | solution.py:155
  548.7 7.0 convolution_bitcast_fusion
  555.7 8.5 %multiply_convert_fusion = bf16[32,2,32,2048]{3,2,1,0:T(8,128)(2,1)} fusion(f32[2]{0:T(128)S(1)} %compare_convert_fusion, f32[32,32,2048]{2,1,0:T(8,128)} %convolution_bitcast_fusion), kind=kLoop, calls=%fused_computation.4 | loop fusion | flops 8388608 | bytes 16777224 | tf_op jit(solution)/shard_map/convert_element_type | solution.py:163
  564.3 93.5 %reduce-scatter.2.cloned.1.call-done = bf16[32,2,32,256]{3,2,1,0:T(8,128)(2,1)} async-done(((bf16[32,2,32,2048]{3,2,1,0:T(8,128)(2,1)}), bf16[32,2,32,256]{3,2,1,0:T(8,128)(2,1)}) %reduce-scatter.2.cloned.1.call-update) | async-done | bytes 1048592 | tf_op jit(solution)/shard_map/reduce_scatter | solution.py:163
  657.8 10.3 %all-to-all-start.1 = ((bf16[32,2,32,256]{3,2,1,0:T(8,128)(2,1)}), bf16[32,2,32,256]{3,2,1,0:T(8,128)(2,1)S(1)}, u32[]{:S(2)}, u32[]{:S(2)}) async-start(bf16[32,2,32,256]{3,2,1,0:T(8,128)(2,1)} %reduce-scatter.2.cloned.1.call-done), calls=%async_computation.2 | async-start | bytes 2097152 | tf_op jit(solution)/shard_map/all_to_all | solution.py:164
  668.1 0.1 copy.59
  668.3 0.1 reshape.336
  668.5 0.4 fusion.67
  668.9 12.7 %gather_fusion.1 = f32[1536]{0:T(1024)S(1)} fusion(f32[256,64]{0,1:T(8,128)S(1)} %fusion.67, s32[1536]{0:T(1024)S(1)} %reshape.336), kind=kCustom, calls=%fused_computation.1 | custom fusion | bytes 24576 | tf_op jit(solution)/shard_map/jit(take_along_axis)/gather | solution.py:115
  681.6 0.1 reshape.339
  681.9 0.1 copy.61
  682.0 15.0 %all-to-all-done.1 = bf16[32,2,32,256]{3,2,1,0:T(8,128)(2,1)S(1)} async-done(((bf16[32,2,32,256]{3,2,1,0:T(8,128)(2,1)}), bf16[32,2,32,256]{3,2,1,0:T(8,128)(2,1)S(1)}, u32[]{:S(2)}, u32[]{:S(2)}) %all-to-all-start.1) | async-done | bytes 1048608 | tf_op jit(solution)/shard_map/all_to_all | solution.py:164
  697.1 4.8 gather_fusion
  701.8 0.2 reshape.327
  702.0 0.7 multiply_reduce_fusion
  702.8 1.6 add_convert_fusion
  (50 shorter events, 0.9 us)
Async XLA Ops:
  6.5 661.9 %copy-start = (bf16[2048,64]{0,1:T(8,128)(2,1)S(1)}, bf16[2048,64]{0,1:T(8,128)(2,1)}, u32[]{:S(2)}) copy-start(bf16[2048,64]{0,1:T(8,128)(2,1)} %param.23) | copy-start | bytes 786436
  6.5 45.5 %all-gather.6.cloned.1.call-start = ((), (), s32[]{:S(2)}) async-start(), calls=%async_computation.3 | async-start | bytes 1179648 | tf_op jit(solution)/shard_map/all_gather | solution.py:79
  7.3 130.2 %all-gather.8.cloned.1.call-start = ((), (), s32[]{:S(2)}) async-start(), calls=%async_computation.4 | async-start | bytes 3244032 | tf_op jit(solution)/shard_map/all_gather | solution.py:83
  8.9 206.1 %all-gather.10.cloned.1.call-start = ((), (), s32[]{:S(2)}) async-start(), calls=%async_computation.5 | async-start | bytes 1081344 | tf_op jit(solution)/shard_map/all_gather | solution.py:84
  10.4 300.5 %all-gather.12.cloned.1.call-start = ((), (), s32[]{:S(2)}) async-start(), calls=%async_computation.7 | async-start | bytes 9437184 | tf_op jit(solution)/shard_map/all_gather | solution.py:109
  27.2 2.8 copy-start.6
  53.5 88.7 %copy-start.2 = (bf16[256,2048]{1,0:T(8,128)(2,1)S(1)}, bf16[256,2048]{1,0:T(8,128)(2,1)}, u32[]{:S(2)}) copy-start(bf16[256,2048]{1,0:T(8,128)(2,1)} %all-gather.6.cloned.1.call-done) | copy-start | bytes 3145732
  53.5 88.6 %copy-start.9 = (f32[2048]{0:T(1024)S(1)}, f32[2048]{0:T(1024)}, u32[]{:S(2)}) copy-start(f32[2048]{0:T(1024)} %param.19) | copy-start | bytes 24580
  145.2 0.9 copy-start.4
  158.2 59.7 %copy-start.5 = (s32[256,6]{0,1:T(8,128)S(1)}, s32[256,6]{0,1:T(8,128)}, u32[]{:S(2)}) copy-start(s32[256,6]{0,1:T(8,128)} %param.24) | copy-start | bytes 18436
  316.1 1.5 copy-start.7
  316.7 1.0 copy-start.1
  348.9 192.5 %all-to-all-start = ((bf16[32,2,32,2048]{3,2,1,0:T(8,128)(2,1)}), bf16[32,2,32,2048]{3,2,1,0:T(8,128)(2,1)}, u32[]{:S(2)}, u32[]{:S(2)}) async-start(bf16[32,2,32,2048]{3,2,1,0:T(8,128)(2,1)} %bitcast.88), calls=%async_computation | async-start | bytes 16777216 | tf_op jit(solution)/shard_map/all_to_all | solution.py:133
  359.1 5.7 copy-start.10
  359.1 298.7 %reduce-scatter.2.cloned.1.call-start = ((), (), s32[]{:S(2)}) async-start(), calls=%async_computation.6 | async-start | bytes 9437184 | tf_op jit(solution)/shard_map/reduce_scatter | solution.py:163
  359.1 3.4 copy-start.3
  362.4 34.6 %collective-permute-start.1 = (bf16[1,176,2,2048]{3,2,1,0:T(2,128)(2,1)S(1)}, bf16[1,176,2,2048]{3,2,1,0:T(2,128)(2,1)}, u32[]{:S(2)}, u32[]{:S(2)}) collective-permute-start(bf16[1,176,2,2048]{3,2,1,0:T(2,128)(2,1)S(1)} %convert_element_type.113), channel_id=1, source_target_pairs={{0,1},{1,0},{2,3},{3,2},{4,5},{5,4},{6,7},{7,6},{8,9},{9,8},{10,11... | collective-permute-start | bytes 4325384 | tf_op jit(solution)/shard_map/ppermute | solution.py:12
  362.6 186.0 %collective-permute-start = (bf16[1,176,2048]{2,1,0:T(8,128)(2,1)S(1)}, bf16[1,176,2048]{2,1,0:T(8,128)(2,1)}, u32[]{:S(2)}, u32[]{:S(2)}) collective-permute-start(bf16[1,176,2048]{2,1,0:T(8,128)(2,1)S(1)} %convert_element_type.112), channel_id=1, source_target_pairs={{0,1},{1,0},{2,3},{3,2},{4,5},{5,4},{6,7},{7,6},{8,9},{9,8},{10,11... | collective-permute-start | bytes 2162696 | tf_op jit(solution)/shard_map/ppermute | solution.py:12
  413.1 135.6 %copy-start.8 = (bf16[1,352,2048]{2,1,0:T(8,128)(2,1)S(1)}, bf16[1,352,2048]{2,1,0:T(8,128)(2,1)}, u32[]{:S(2)}) copy-start(bf16[1,352,2048]{2,1,0:T(8,128)(2,1)} %param.29) | copy-start | bytes 4325380
  657.8 39.3 %all-to-all-start.1 = ((bf16[32,2,32,256]{3,2,1,0:T(8,128)(2,1)}), bf16[32,2,32,256]{3,2,1,0:T(8,128)(2,1)S(1)}, u32[]{:S(2)}, u32[]{:S(2)}) async-start(bf16[32,2,32,256]{3,2,1,0:T(8,128)(2,1)} %reduce-scatter.2.cloned.1.call-done), calls=%async_computation.2 | async-start | bytes 2097152 | tf_op jit(solution)/shard_map/all_to_all | solution.py:164
Sparse Core Ops, SparseCore 0:
  9.1 42.8 all-gather.5
  54.8 82.6 all-gather.7
  140.3 74.7 all-gather.9
  218.0 92.9 all-gather.11
  564.4 93.3 reduce-scatter.1
